TPU v7x, 32 devices: a whole 2x2x4 slice. The times are simulated.
32 devices in a mesh: hid: 8 (over y, x, core), ep: 4 (over z).
Axes of the slice: x: 2, y: 2, z: 4, core: 2. Of those that a mesh axis runs over, the one named last changes fastest.
Arguments:
- tokens: bfloat16 [2048, 2048], P('ep', 'hid'), may hold values from -6 to 6
- expert_ids: int32 [2048, 6], P('ep'), may hold values from 0 to 15, all different within a row; in each aligned block of 512 rows (0 to 511, 512 to 1023, ...) at most 256 rows name the same one
- gate_weights: float32 [2048, 6], P('ep'), may hold values from 0.1 to 1
- w_gate_up: bfloat16 [4, 5632, 2, 2048], P('ep', 'hid'), may hold values from -0.125 to 0.125
- w_down: bfloat16 [4, 5632, 2048], P('ep', 'hid'), may hold values from -0.21875 to 0.21875
Outputs:
- mixed: bfloat16 [2048, 2048], P('ep', 'hid')
Inputs may be any that keep to these rules, and one draw needn't show every extreme that they name: `expert_ids`: the 6 ids of a row differ. Among the 512 rows of one index of ep (aligned blocks of rows), no expert is named by more than 256 rows.
All inputs are finite; a program needn't handle non-finite values.
Results may differ from a plain program's by a relative error of at most 0.0064.
Values may be sent and summed in bfloat16 or wider, within the bound.
A program may use at most 64 MiB of HBM per device.

v0:
```python
import jax
import jax.numpy as jnp
from jax import lax
from jax.sharding import PartitionSpec as P

EXP_DEV = 4


def slot_numbers(ids, count):
    flat = ids.reshape(-1)
    onehot = (flat[:, None] == jnp.arange(count, dtype=jnp.int32)[None, :]).astype(jnp.int32)
    before = jnp.cumsum(onehot, axis=0) - onehot
    return jnp.sum(before * onehot, axis=1).reshape(ids.shape)


def on_device(tokens, expert_ids, gate_weights, w_gate_up, w_down):
    groups = lax.axis_size("ep")
    hid_count = lax.axis_size("hid")
    shards = hid_count // EXP_DEV
    experts = EXP_DEV * groups
    tok_rows = tokens.shape[0]
    width_local = tokens.shape[1]
    topk = expert_ids.shape[1]
    capacity = tok_rows * topk * 4 // (3 * experts)
    rows_per = groups * capacity
    slot = slot_numbers(expert_ids, experts)
    token_index = jnp.broadcast_to(jnp.arange(tok_rows, dtype=jnp.int32)[:, None], expert_ids.shape)
    table = (
        jnp.full((experts, capacity), tok_rows, dtype=jnp.int32)
        .at[expert_ids, slot]
        .set(token_index)
    )
    padded = jnp.concatenate([tokens, jnp.zeros((1, width_local), tokens.dtype)], axis=0)
    placed = padded[table].reshape(groups, EXP_DEV, capacity, width_local)
    arrived = lax.all_to_all(placed, "ep", split_axis=0, concat_axis=2, tiled=True)[0]
    repeated = jnp.repeat(arrived, shards, axis=0)
    outgoing = jnp.transpose(repeated, (1, 0, 2)).reshape(rows_per, hid_count * width_local)
    full_rows = lax.all_to_all(outgoing, "hid", split_axis=1, concat_axis=1, tiled=True)
    gate_up = jnp.einsum("rd,fgd->gfr", full_rows, w_gate_up[0], preferred_element_type=jnp.float32)
    hidden = (jax.nn.silu(gate_up[0]) * gate_up[1]).astype(jnp.bfloat16)
    partial_value = jnp.einsum("fr,fd->rd", hidden, w_down[0], preferred_element_type=jnp.float32)
    rounded = partial_value.astype(jnp.bfloat16)
    homed = lax.all_to_all(
        rounded.reshape(1, groups, capacity, rounded.shape[1]),
        "ep",
        split_axis=1,
        concat_axis=0,
        tiled=True,
    )
    moved = lax.all_to_all(homed, "hid", split_axis=3, concat_axis=0, tiled=True)
    grouped = moved.reshape(EXP_DEV, shards, groups, capacity, width_local).astype(jnp.float32)
    summed = jnp.sum(grouped, axis=1).astype(jnp.bfloat16)
    back = jnp.transpose(summed, (1, 0, 2, 3))
    flat = back.reshape(experts * capacity, width_local)
    picked = flat[expert_ids * capacity + slot]
    mixed = jnp.sum(picked.astype(jnp.float32) * gate_weights[:, :, None], axis=1)
    return mixed.astype(jnp.bfloat16)


def solution(mesh):
    return jax.shard_map(
        on_device,
        mesh=mesh,
        in_specs=(
            P("ep", "hid"),
            P("ep", None),
            P("ep", None),
            P("ep", "hid", None, None),
            P("ep", "hid", None),
        ),
        out_specs=P("ep", "hid"),
        check_vma=False,
    )
```

profile of v0, /device:TPU:0, one launch (start us, length us, event | category | flops | bytes accessed | tf_op | source)
XLA Modules:
  0.0 363.1 jit_solution(8262749961850203869)
XLA Ops:
  0.0 0.0 copy-start
  0.0 0.0 copy-start.5
  0.0 0.0 copy-start.4
  0.0 0.0 copy-start.2
  0.0 1.0 copy.60
  1.0 0.2 eq.29
  1.2 0.2 eq.25
  1.4 4.6 %reduce-window.6 = s32[16,24,128]{2,1,0:T(8,128)S(1)} reduce-window(s32[16,24,128]{2,1,0:T(8,128)S(1)} %fusion.12, s32[]{:T(128)} %constant.5.clone.1), window={size=1x1x128 pad=0_0x0_0x127_0}, to_apply=%region_0.0 | reduce-window | flops 6242304 | bytes 393220 | tf_op jit(solution)/shard_map/reduce-window
  6.0 0.4 slice_reduce_fusion
  6.4 0.2 reduce-window.9
  6.6 0.1 broadcast_add_fusion
  6.8 0.1 fusion.11
  6.8 0.2 reshape.83
  7.0 0.2 reshape.77
  7.3 0.1 copy.72
  7.4 0.0 copy-done.2
  7.5 0.1 copy.63
  7.6 0.0 copy-done.5
  7.6 0.1 multiply_reduce_fusion.1
  7.7 0.0 copy-done.4
  7.7 0.1 and_reduce_fusion
  7.8 0.1 copy.64
  8.0 0.2 reshape.104
  8.2 0.2 reshape.106
  8.3 11.8 %scatter_custom_fusion = s32[4096]{0:T(1024)S(1)} fusion(s32[3072]{0:T(1024)S(1)} %reshape.104, s32[3072]{0:T(1024)S(1)} %reshape.106, s32[]{:T(128)} %constant.10.clone.1), kind=kCustom, calls=%fused_computation.31 | custom fusion | bytes 16388
  20.2 1.0 concatenate.6
  21.2 16.9 %gather_fusion = bf16[4096,256]{1,0:T(8,128)(2,1)} fusion(bf16[513,256]{1,0:T(8,128)(2,1)S(1)} %concatenate.6, s32[4096]{0:T(1024)S(1)} %broadcast_clamp_fusion), kind=kCustom, calls=%fused_computation | custom fusion | bytes 4210688 | tf_op jit(solution)/shard_map/gather | solution.py:34
  38.1 54.5 %all_to_all.51 = bf16[4,4,256,256]{3,2,1,0:T(8,128)(2,1)S(1)} all-to-all(bf16[4,4,256,256]{3,2,1,0:T(8,128)(2,1)} %bitcast.59), channel_id=1, replica_groups=mesh['hid'=8,'ep'=4] {'ep'}, dimensions={0} | all-to-all | bytes 4194304 | tf_op jit(solution)/shard_map/all_to_all | solution.py:35
  92.6 0.1 copy.65
  92.8 0.3 broadcast_in_dim.29
  93.1 52.6 %all_to_all.52 = bf16[1024,8,256]{2,0,1:T(8,128)(2,1)S(1)} all-to-all(bf16[1024,8,256]{2,0,1:T(8,128)(2,1)S(1)} %bitcast.55), channel_id=1, replica_groups=mesh['hid'=8,'ep'=4] {'hid'}, dimensions={1} | all-to-all | bytes 8388608 | tf_op jit(solution)/shard_map/all_to_all | solution.py:38
  145.6 4.3 %copy.66 = bf16[1024,8,256]{2,1,0:T(8,128)(2,1)} copy(bf16[1024,8,256]{2,0,1:T(8,128)(2,1)S(1)} %all_to_all.52) | data formatting | bytes 8388608 | tf_op jit(solution)/shard_map/all_to_all | solution.py:38
  150.0 7.4 %reshape.116 = bf16[1024,2048,1]{1,0,2:T(8,128)(2,1)} reshape(bf16[1024,8,256]{2,1,0:T(8,128)(2,1)} %copy.66) | data formatting | bytes 8388608 | tf_op jit(solution)/shard_map/all_to_all | solution.py:38
  157.4 12.0 %fusion.4 = f32[2,704,1024]{2,1,0:T(8,128)S(1)} fusion(bf16[1024,2048,1]{1,0,2:T(8,128)(2,1)} %reshape.116, bf16[704,2,2048]{2,1,0:T(2,128)(2,1)} %bitcast.64), kind=kOutput, calls=%fused_computation.10 | convolution fusion | flops 5905580032 | bytes 15728640 | tf_op jit(solution)/shard_map/rd,fgd->gfr/dot_general | solution.py:39
  169.4 0.0 copy-done
  169.4 3.9 %convolution_convert_fusion = bf16[1024,2048]{1,0:T(8,128)(2,1)S(1)} fusion(bf16[1,704,2048]{2,1,0:T(8,128)(2,1)S(1)} %copy-done, f32[2,704,1024]{2,1,0:T(8,128)S(1)} %fusion.4), kind=kOutput, calls=%fused_computation.6 | convolution fusion | flops 2959212544 | bytes 12845056 | tf_op jit(solution)/shard_map/fr,fd->rd/dot_general | solution.py:41
  173.3 96.3 %all_to_all.53 = bf16[1,4,256,2048]{3,2,0,1:T(8,128)(2,1)} all-to-all(bf16[1,4,256,2048]{3,2,0,1:T(8,128)(2,1)S(1)} %bitcast.60), channel_id=1, replica_groups=mesh['hid'=8,'ep'=4] {'ep'}, dimensions={1} | all-to-all | bytes 8388608 | tf_op jit(solution)/shard_map/all_to_all | solution.py:43
  269.6 7.5 %copy.69 = bf16[4,1,256,2048]{2,0,1,3:T(4,128)(2,1)} copy(bf16[4,1,256,2048]{3,2,0,1:T(8,128)(2,1)} %bitcast.56) | data formatting | bytes 8388608 | tf_op jit(solution)/shard_map/all_to_all | solution.py:43
  277.1 0.0 copy-start.3
  277.1 4.9 %all-to-all-start.3 = ((bf16[4,1,256,2048]{2,0,1,3:T(4,128)(2,1)}), bf16[4,1,256,2048]{2,0,1,3:T(4,128)(2,1)}, u32[]{:S(2)}, u32[]{:S(2)}) async-start(bf16[4,1,256,2048]{2,0,1,3:T(4,128)(2,1)} %copy.69), calls=%async_computation.3 | async-start | bytes 8388608 | tf_op jit(solution)/shard_map/all_to_all | solution.py:50
  282.0 0.1 copy.73
  282.1 0.2 reshape.98
  282.3 0.0 copy-done.3
  282.3 0.1 copy.74
  282.5 48.4 %all-to-all-done.3 = bf16[4,1,256,2048]{2,0,1,3:T(4,128)(2,1)} async-done(((bf16[4,1,256,2048]{2,0,1,3:T(4,128)(2,1)}), bf16[4,1,256,2048]{2,0,1,3:T(4,128)(2,1)}, u32[]{:S(2)}, u32[]{:S(2)}) %all-to-all-start.3) | async-done | bytes 4194336 | tf_op jit(solution)/shard_map/all_to_all | solution.py:50
  330.9 6.9 %reduce_sum.31 = bf16[4,4,256,256]{2,1,3,0:T(4,128)(2,1)} reduce(bf16[4,2,4,256,256]{3,2,4,1,0:T(4,128)(2,1)} %bitcast.17, bf16[]{:T(256)} %constant.9.clone.1), dimensions={1}, to_apply=%region_4.5 | reduce | flops 1048576 | bytes 6291458 | tf_op jit(solution)/shard_map/reduce_sum | solution.py:52
  337.8 3.0 copy.71
  340.8 13.0 %gather_fusion.1 = bf16[3072,256]{1,0:T(8,128)(2,1)} fusion(bf16[4096,256]{1,0:T(8,128)(2,1)S(1)} %bitcast.54, s32[3072]{0:T(1024)S(1)} %broadcast_clamp_fusion.1), kind=kCustom, calls=%fused_computation.1 | custom fusion | bytes 3158016 | tf_op jit(solution)/shard_map/gather | solution.py:55
  353.8 0.0 copy-start.1
  353.8 4.1 %reshape.115 = f32[512,6,256]{2,1,0:T(8,128)} reshape(bf16[3072,256]{1,0:T(8,128)(2,1)} %gather_fusion.1) | data formatting | bytes 4718592 | tf_op jit(solution)/shard_map/convert_element_type | solution.py:56
  357.9 5.2 %multiply_reduce_fusion = bf16[512,256]{1,0:T(8,128)(2,1)} fusion(f32[512,6,256]{2,1,0:T(8,128)} %reshape.115, f32[512,6]{1,0:T(8,128)S(1)} %copy.74), kind=kLoop, calls=%fused_computation.5 | loop fusion | flops 1441792 | bytes 3420160 | tf_op jit(solution)/shard_map/reduce_sum | solution.py:56
  363.1 0.0 copy-done.1
  (11 shorter events, 0.1 us)
Async XLA Ops:
  0.0 169.4 %copy-start = (bf16[1,704,2048]{2,1,0:T(8,128)(2,1)S(1)}, bf16[1,704,2048]{2,1,0:T(8,128)(2,1)}, u32[]{:S(2)}) copy-start(bf16[1,704,2048]{2,1,0:T(8,128)(2,1)} %param.9) | copy-start | bytes 8650756
  0.0 7.6 %copy-start.5 = (s32[2]{0:T(128)S(1)}, s32[2]{0:T(128)}, u32[]{:S(2)}) copy-start(s32[2]{0:T(128)} %constant.30) | copy-start | bytes 28
  0.0 7.7 %copy-start.4 = (s32[2]{0:T(128)S(1)}, s32[2]{0:T(128)}, u32[]{:S(2)}) copy-start(s32[2]{0:T(128)} %constant.33) | copy-start | bytes 28
  0.0 7.4 %copy-start.2 = (s32[512,6]{0,1:T(8,128)S(1)}, s32[512,6]{0,1:T(8,128)}, u32[]{:S(2)}) copy-start(s32[512,6]{0,1:T(8,128)} %param.6) | copy-start | bytes 36868
  277.1 5.2 %copy-start.3 = (f32[512,6]{0,1:T(8,128)S(1)}, f32[512,6]{0,1:T(8,128)}, u32[]{:S(2)}) copy-start(f32[512,6]{0,1:T(8,128)} %param.7) | copy-start | bytes 36868
  277.1 53.8 %all-to-all-start.3 = ((bf16[4,1,256,2048]{2,0,1,3:T(4,128)(2,1)}), bf16[4,1,256,2048]{2,0,1,3:T(4,128)(2,1)}, u32[]{:S(2)}, u32[]{:S(2)}) async-start(bf16[4,1,256,2048]{2,0,1,3:T(4,128)(2,1)} %copy.69), calls=%async_computation.3 | async-start | bytes 8388608 | tf_op jit(solution)/shard_map/all_to_all | solution.py:50
  353.8 9.3 %copy-start.1 = (bf16[1,704,2048]{2,1,0:T(8,128)(2,1)S(1)}, bf16[1,704,2048]{2,1,0:T(8,128)(2,1)}, u32[]{:S(2)}) copy-start(bf16[1,704,2048]{2,1,0:T(8,128)(2,1)} %param.9) | copy-start | bytes 8650756
where the time goes:
time: 364 us; the launch traced here: 363 us
  blocking collectives  203 us (56%)
  local copies, waits for them, and re-layouts  72.8 us (20%)
  waiting for transfers between devices  48.4 us (13%)
  other arithmetic  17.4 us (5%)
  matrix products  15.9 us (4%)
  starting transfers between devices  4.9 us (1%)
    all_to_all x1, blocking collectives, on_device(): lax.all_to_all(rounded.reshape(1, groups, capacity, rounded.shape[1]), 'e...  96.3 us
    all_to_all x1, blocking collectives, on_device(): lax.all_to_all(placed, 'ep', split_axis=0, concat_axis=2, tiled=True)[0]  54.5 us
    all_to_all x1, blocking collectives, on_device(): lax.all_to_all(outgoing, 'hid', split_axis=1, concat_axis=1, tiled=True)  52.6 us
    all_to_all x1, waiting for transfers between devices, on_device(): lax.all_to_all(homed, 'hid', split_axis=3, concat_axis=0, tiled=True)  48.4 us
    gather x1, local copies, waits for them, and re-layouts, on_device(): placed = padded[table].reshape(groups, EXP_DEV, capacity, width_local)  16.9 us
    unnamed x18, local copies, waits for them, and re-layouts  13.3 us
    gather x1, local copies, waits for them, and re-layouts, on_device(): picked = flat[expert_ids * capacity + slot]  13 us
    dot_general x1, matrix products, on_device(): jnp.einsum('rd,fgd->gfr', full_rows, w_gate_up[0], preferred_element_type...  12 us
  transfers between devices with their start and end apart: 1, of which 1 were waited for; matrix products, arithmetic and copies ran while one was open for 0% of the time, Pallas kernels for 0%

commit v1 on v0

--- a/solution.py
+++ b/solution.py
@@ -35,7 +35,10 @@
     arrived = lax.all_to_all(placed, "ep", split_axis=0, concat_axis=2, tiled=True)[0]
     repeated = jnp.repeat(arrived, shards, axis=0)
     outgoing = jnp.transpose(repeated, (1, 0, 2)).reshape(rows_per, hid_count * width_local)
-    full_rows = lax.all_to_all(outgoing, "hid", split_axis=1, concat_axis=1, tiled=True)
+    full_rows = jnp.concatenate(
+        lax.all_to_all(jnp.stack(jnp.split(outgoing, lax.axis_size("hid"), axis=1)), "hid", 0, 0),
+        axis=1,
+    )
     gate_up = jnp.einsum("rd,fgd->gfr", full_rows, w_gate_up[0], preferred_element_type=jnp.float32)
     hidden = (jax.nn.silu(gate_up[0]) * gate_up[1]).astype(jnp.bfloat16)
     partial_value = jnp.einsum("fr,fd->rd", hidden, w_down[0], preferred_element_type=jnp.float32)

time: 364 us -> 385 us (1.058)
  local copies, waits for them, and re-layouts: 72.8 us -> 91.7 us
    reshape x0 -> x3, local copies, waits for them, and re-layouts: none -> 18.9 us  [the longest x2 11.7 us: on_device(): jnp.concatenate(lax.all_to_all(jnp.stack(jnp.split(outgoing, lax.axis_siz...]
    all_to_all x2 -> x0, local copies, waits for them, and re-layouts: 11.7 us -> none  [on_device(): lax.all_to_all(outgoing, 'hid', split_axis=1, concat_axis=1, tiled=True)]
    unnamed x18, local copies, waits for them, and re-layouts: 13.3 us -> 17.4 us
where the time goes in v1:
time: 385 us; the launch traced here: 384 us
  blocking collectives  203 us (53%)
  local copies, waits for them, and re-layouts  91.7 us (24%)
  waiting for transfers between devices  48.4 us (13%)
  other arithmetic  19.4 us (5%)
  matrix products  15.9 us (4%)
  starting transfers between devices  4.9 us (1%)
    all_to_all x1, blocking collectives, on_device(): lax.all_to_all(rounded.reshape(1, groups, capacity, rounded.shape[1]), 'e...  96.3 us
    all_to_all x1, blocking collectives, on_device(): lax.all_to_all(placed, 'ep', split_axis=0, concat_axis=2, tiled=True)[0]  54.5 us
    all_to_all x1, blocking collectives, on_device(): lax.all_to_all(jnp.stack(jnp.split(outgoing, lax.axis_size('hid'), axis=1...  52.6 us
    all_to_all x1, waiting for transfers between devices, on_device(): lax.all_to_all(homed, 'hid', split_axis=3, concat_axis=0, tiled=True)  48.4 us
    unnamed x18, local copies, waits for them, and re-layouts  17.4 us
    gather x1, local copies, waits for them, and re-layouts, on_device(): placed = padded[table].reshape(groups, EXP_DEV, capacity, width_local)  16.9 us
    gather x1, local copies, waits for them, and re-layouts, on_device(): picked = flat[expert_ids * capacity + slot]  14 us
    dot_general x1, matrix products, on_device(): jnp.einsum('rd,fgd->gfr', full_rows, w_gate_up[0], preferred_element_type...  12 us
  transfers between devices with their start and end apart: 1, of which 1 were waited for; matrix products, arithmetic and copies ran while one was open for 0% of the time, Pallas kernels for 0%

profile of v1, /device:TPU:0, one launch (start us, length us, event | category | flops | bytes accessed | tf_op | source)
XLA Modules:
  0.0 384.0 jit_solution(2429572062552008125)
XLA Ops:
  0.0 0.0 copy-start
  0.0 1.0 copy.70
  1.0 0.2 eq.29
  1.2 0.2 eq.25
  1.4 4.6 %reduce-window.6 = s32[16,24,128]{2,1,0:T(8,128)S(1)} reduce-window(s32[16,24,128]{2,1,0:T(8,128)S(1)} %fusion.20, s32[]{:T(128)} %constant.5.clone.1), window={size=1x1x128 pad=0_0x0_0x127_0}, to_apply=%region_0.0 | reduce-window | flops 6242304 | bytes 393220 | tf_op jit(solution)/shard_map/reduce-window
  6.0 0.4 slice_reduce_fusion
  6.4 0.2 reduce-window.9
  6.6 0.1 broadcast_add_fusion
  6.7 0.1 fusion.19
  6.8 0.2 reshape.91
  7.0 0.2 reshape.82
  7.2 0.1 copy.83
  7.3 0.7 compare_select_fusion.1
  8.1 0.1 copy.73
  8.2 0.8 multiply_reduce_fusion.1
  9.0 0.8 and_reduce_fusion
  9.8 0.1 copy.74
  10.0 0.2 reshape.112
  10.2 0.2 reshape.114
  10.3 11.8 %scatter_custom_fusion = s32[4096]{0:T(1024)S(1)} fusion(s32[3072]{0:T(1024)S(1)} %reshape.112, s32[3072]{0:T(1024)S(1)} %reshape.114, s32[]{:T(128)} %constant.10.clone.1), kind=kCustom, calls=%fused_computation.47 | custom fusion | bytes 16388
  22.2 1.0 concatenate.6
  23.2 16.9 %gather_fusion = bf16[4096,256]{1,0:T(8,128)(2,1)} fusion(bf16[513,256]{1,0:T(8,128)(2,1)S(1)} %concatenate.6, s32[4096]{0:T(1024)S(1)} %broadcast_clamp_fusion), kind=kCustom, calls=%fused_computation | custom fusion | bytes 4210688 | tf_op jit(solution)/shard_map/gather | solution.py:34
  40.1 54.5 %all_to_all.47 = bf16[4,4,256,256]{3,2,1,0:T(8,128)(2,1)S(1)} all-to-all(bf16[4,4,256,256]{3,2,1,0:T(8,128)(2,1)} %bitcast.103), channel_id=1, replica_groups=mesh['hid'=8,'ep'=4] {'ep'}, dimensions={0} | all-to-all | bytes 4194304 | tf_op jit(solution)/shard_map/all_to_all | solution.py:35
  94.6 0.1 copy.75
  94.8 1.6 copy.76
  96.4 3.9 %broadcast_in_dim.29 = bf16[4,2,1024,256]{3,1,0,2:T(2,128)(2,1)} broadcast(bf16[4,1024,256]{2,0,1:T(4,128)(2,1)S(1)} %copy.76), dimensions={0,2,3} | broadcast | bytes 6291456 | tf_op jit(solution)/shard_map/broadcast_in_dim | solution.py:36
  100.3 7.2 %reshape.84 = bf16[8,1024,256]{2,0,1:T(8,128)(2,1)} reshape(bf16[4,2,1024,256]{3,1,0,2:T(2,128)(2,1)} %broadcast_in_dim.29) | data formatting | bytes 8388608 | tf_op jit(solution)/shard_map/reshape | solution.py:36
  107.5 3.7 copy.91
  111.2 0.1 fusion.16
  111.3 0.1 fusion.15
  111.4 0.1 fusion.14
  111.4 0.1 fusion.13
  111.5 0.1 fusion.12
  111.6 0.1 fusion.11
  111.7 0.1 fusion.10
  111.8 0.1 fusion.9
  111.8 52.6 %all_to_all.48 = bf16[8,1024,256]{2,1,0:T(8,128)(2,1)S(1)} all-to-all(bf16[8,1024,256]{2,1,0:T(8,128)(2,1)S(1)} %fusion.9), channel_id=1, replica_groups=mesh['hid'=8,'ep'=4] {'hid'}, dimensions={0} | all-to-all | bytes 8388608 | tf_op jit(solution)/shard_map/all_to_all | solution.py:39
  164.4 4.3 %copy.77 = bf16[1024,8,256]{2,1,0:T(8,128)(2,1)} copy(bf16[1024,8,256]{2,0,1:T(8,128)(2,1)S(1)} %bitcast.99) | data formatting | bytes 8388608 | tf_op jit(solution)/shard_map/reshape | solution.py:38
  168.7 7.4 %reshape.124 = bf16[1024,2048,1]{1,0,2:T(8,128)(2,1)} reshape(bf16[1024,8,256]{2,1,0:T(8,128)(2,1)} %copy.77) | data formatting | bytes 8388608 | tf_op jit(solution)/shard_map/reshape | solution.py:38
  176.1 12.0 %fusion.4 = f32[2,704,1024]{2,1,0:T(8,128)S(1)} fusion(bf16[1024,2048,1]{1,0,2:T(8,128)(2,1)} %reshape.124, bf16[704,2,2048]{2,1,0:T(2,128)(2,1)} %bitcast.108), kind=kOutput, calls=%fused_computation.10 | convolution fusion | flops 5905580032 | bytes 15728640 | tf_op jit(solution)/shard_map/rd,fgd->gfr/dot_general | solution.py:42
  188.2 0.0 copy-done
  188.2 3.9 %convolution_convert_fusion = bf16[1024,2048]{1,0:T(8,128)(2,1)S(1)} fusion(bf16[1,704,2048]{2,1,0:T(8,128)(2,1)S(1)} %copy-done, f32[2,704,1024]{2,1,0:T(8,128)S(1)} %fusion.4), kind=kOutput, calls=%fused_computation.6 | convolution fusion | flops 2959212544 | bytes 12845056 | tf_op jit(solution)/shard_map/fr,fd->rd/dot_general | solution.py:44
  192.1 96.3 %all_to_all.49 = bf16[1,4,256,2048]{3,2,0,1:T(8,128)(2,1)} all-to-all(bf16[1,4,256,2048]{3,2,0,1:T(8,128)(2,1)S(1)} %bitcast.104), channel_id=1, replica_groups=mesh['hid'=8,'ep'=4] {'ep'}, dimensions={1} | all-to-all | bytes 8388608 | tf_op jit(solution)/shard_map/all_to_all | solution.py:46
  288.4 7.5 %copy.80 = bf16[4,1,256,2048]{2,0,1,3:T(4,128)(2,1)} copy(bf16[4,1,256,2048]{3,2,0,1:T(8,128)(2,1)} %bitcast.100) | data formatting | bytes 8388608 | tf_op jit(solution)/shard_map/all_to_all | solution.py:46
  295.8 0.0 copy-start.1
  295.8 4.9 %all-to-all-start.3 = ((bf16[4,1,256,2048]{2,0,1,3:T(4,128)(2,1)}), bf16[4,1,256,2048]{2,0,1,3:T(4,128)(2,1)}, u32[]{:S(2)}, u32[]{:S(2)}) async-start(bf16[4,1,256,2048]{2,0,1,3:T(4,128)(2,1)} %copy.80), calls=%async_computation.3 | async-start | bytes 8388608 | tf_op jit(solution)/shard_map/all_to_all | solution.py:53
  300.7 0.1 copy.84
  300.9 0.2 reshape.106
  301.1 0.0 copy-done.1
  301.1 0.1 copy.85
  301.2 48.4 %all-to-all-done.3 = bf16[4,1,256,2048]{2,0,1,3:T(4,128)(2,1)} async-done(((bf16[4,1,256,2048]{2,0,1,3:T(4,128)(2,1)}), bf16[4,1,256,2048]{2,0,1,3:T(4,128)(2,1)}, u32[]{:S(2)}, u32[]{:S(2)}) %all-to-all-start.3) | async-done | bytes 4194336 | tf_op jit(solution)/shard_map/all_to_all | solution.py:53
  349.6 6.9 %reduce_sum.31 = bf16[4,4,256,256]{2,1,3,0:T(4,128)(2,1)} reduce(bf16[4,2,4,256,256]{3,2,4,1,0:T(4,128)(2,1)} %bitcast.25, bf16[]{:T(256)} %constant.9.clone.1), dimensions={1}, to_apply=%region_4.5 | reduce | flops 1048576 | bytes 6291458 | tf_op jit(solution)/shard_map/reduce_sum | solution.py:55
  356.5 4.3 %copy.82 = bf16[4,4,256,256]{3,2,1,0:T(8,128)(2,1)} copy(bf16[4,4,256,256]{2,0,3,1:T(4,128)(2,1)} %bitcast.101) | data formatting | bytes 4194304 | tf_op jit(solution)/shard_map/transpose | solution.py:56
  360.8 14.0 %gather_fusion.1 = bf16[3072,256]{1,0:T(8,128)(2,1)} fusion(bf16[4096,256]{1,0:T(8,128)(2,1)} %bitcast.89, s32[3072]{0:T(1024)S(1)} %broadcast_clamp_fusion.1), kind=kCustom, calls=%fused_computation.1 | custom fusion | bytes 3158016 | tf_op jit(solution)/shard_map/gather | solution.py:58
  374.8 4.0 %reshape.123 = f32[512,6,256]{2,1,0:T(8,128)} reshape(bf16[3072,256]{1,0:T(8,128)(2,1)} %gather_fusion.1) | data formatting | bytes 4718592 | tf_op jit(solution)/shard_map/convert_element_type | solution.py:59
  378.8 5.2 %multiply_reduce_fusion = bf16[512,256]{1,0:T(8,128)(2,1)} fusion(f32[512,6,256]{2,1,0:T(8,128)} %reshape.123, f32[512,6]{1,0:T(8,128)S(1)} %copy.85), kind=kLoop, calls=%fused_computation.5 | loop fusion | flops 1441792 | bytes 3420160 | tf_op jit(solution)/shard_map/reduce_sum | solution.py:59
  (10 shorter events, 0.1 us)
Async XLA Ops:
  0.0 188.2 %copy-start = (bf16[1,704,2048]{2,1,0:T(8,128)(2,1)S(1)}, bf16[1,704,2048]{2,1,0:T(8,128)(2,1)}, u32[]{:S(2)}) copy-start(bf16[1,704,2048]{2,1,0:T(8,128)(2,1)} %param.9) | copy-start | bytes 8650756
  295.8 5.2 %copy-start.1 = (f32[512,6]{0,1:T(8,128)S(1)}, f32[512,6]{0,1:T(8,128)}, u32[]{:S(2)}) copy-start(f32[512,6]{0,1:T(8,128)} %param.7) | copy-start | bytes 36868
  295.8 53.8 %all-to-all-start.3 = ((bf16[4,1,256,2048]{2,0,1,3:T(4,128)(2,1)}), bf16[4,1,256,2048]{2,0,1,3:T(4,128)(2,1)}, u32[]{:S(2)}, u32[]{:S(2)}) async-start(bf16[4,1,256,2048]{2,0,1,3:T(4,128)(2,1)} %copy.80), calls=%async_computation.3 | async-start | bytes 8388608 | tf_op jit(solution)/shard_map/all_to_all | solution.py:53
